TPU v7x, 32 devices: a whole 2x2x4 slice. The times are simulated.
32 devices in a mesh: space: 8 (over z, x), filt: 4 (over y, core).
Axes of the slice: x: 2, y: 2, z: 4, core: 2. Of those that a mesh axis runs over, the one named last changes fastest.
Arguments:
- inputs: bfloat16 [16, 4, 32, 512], P('space'), may hold values from -6 to 6
- pre_hidden: bfloat16 [16, 4, 32, 512], P('space'), may hold values from -6 to 6
- weight_one: bfloat16 [512, 3, 3, 3, 512], P(None, None, None, None, 'filt'), may hold values from -0.0546875 to 0.0546875
- weight_two: bfloat16 [512, 3, 3, 3, 512], P(None, None, None, None, 'filt'), may hold values from -0.0546875 to 0.0546875
- grad_out: bfloat16 [16, 4, 32, 512], P('space', None, None, 'filt'), may hold values from -6 to 6
Outputs:
- grad_inputs: bfloat16 [16, 4, 32, 512], P('space', 'filt')
- grad_one: float32 [512, 3, 3, 3, 512], P('space', None, None, None, 'filt')
- grad_two: float32 [512, 3, 3, 3, 512], P('space', None, None, None, 'filt')
All inputs are finite; a program needn't handle non-finite values.
Results may differ from a plain program's by a relative error of at most 0.0049.
Values may be sent and summed in bfloat16 or wider, within the bound.
A program may use at most 128 MiB of HBM per device.

v0:
```python
import math
import jax
import jax.numpy as jnp
from jax import lax
from jax.sharding import PartitionSpec as P

TAP_LIST = [
    (tap_depth, tap_row, tap_col)
    for tap_depth in range(3)
    for tap_row in range(3)
    for tap_col in range(3)
]


def window_at(padded, tap, planes, height, columns):
    return padded[
        2 - tap[0] : 2 - tap[0] + planes,
        2 - tap[1] : 2 - tap[1] + height,
        2 - tap[2] : 2 - tap[2] + columns,
        :,
    ]


def carry_back(padded, weight, planes, height, columns):
    channels = weight.shape[4]
    summed = jnp.zeros((planes * height * columns, weight.shape[0]), jnp.float32)
    for tap in TAP_LIST:
        window = window_at(padded, tap, planes, height, columns).reshape(-1, channels)
        summed = summed + lax.dot_general(
            window,
            weight[:, tap[0], tap[1], tap[2], :],
            (((1,), (1,)), ((), ())),
            preferred_element_type=jnp.float32,
        )
    return summed.reshape(planes, height, columns, weight.shape[0])


def weight_terms(source, padded, planes, height, columns, factor):
    channels = padded.shape[3]
    pieces = []
    for tap in TAP_LIST:
        window = window_at(padded, tap, planes, height, columns).reshape(-1, channels)
        pieces.append(
            lax.dot_general(
                source, window, (((1,), (0,)), ((), ())), preferred_element_type=jnp.float32
            )
            * factor
        )
    return jnp.stack(pieces, axis=1).reshape(source.shape[0], 3, 3, 3, channels)


def pad_all(field):
    return jnp.pad(field, ((1, 1), (1, 1), (1, 1), (0, 0)))


def shards(inputs, pre_hidden, weight_one, weight_two, grad_out):
    planes, height, columns, in_channels = inputs.shape
    mid_channels = pre_hidden.shape[3]
    count = lax.axis_size("space")
    voxel_local = planes * height * columns
    factor = 1.0 / math.sqrt(voxel_local * count)
    start = lax.axis_index("space") * planes
    out_all = pad_all(lax.all_gather(grad_out, "space", axis=0, tiled=True))
    out_pad = lax.dynamic_slice_in_dim(out_all, start, planes + 2, 0)
    activity = jnp.maximum(pre_hidden, jnp.zeros_like(pre_hidden))
    both = jnp.stack([activity, inputs]).reshape(2, voxel_local, in_channels)
    both = jnp.swapaxes(both, 1, 2).reshape(2, count, in_channels // count, voxel_local)
    both = lax.all_to_all(both, "space", 1, 1)
    both = jnp.swapaxes(both, 1, 2).reshape(2, in_channels // count, count * voxel_local)
    hidden_partial = carry_back(out_pad, weight_two, planes, height, columns)
    grad_hidden = lax.psum_scatter(hidden_partial, "filt", scatter_dimension=3, tiled=True)
    group_width = grad_hidden.shape[3]
    own_pre = lax.dynamic_slice_in_dim(
        pre_hidden, lax.axis_index("filt") * group_width, group_width, 3
    )
    grad_pre = jnp.where(own_pre > 0, grad_hidden, jnp.zeros_like(grad_hidden)).astype(jnp.bfloat16)
    pre_all = pad_all(lax.all_gather(grad_pre, "space", axis=0, tiled=True))
    pre_pad = lax.dynamic_slice_in_dim(pre_all, start, planes + 2, 0)
    input_partial = carry_back(pre_pad, weight_one, planes, height, columns)
    grad_rows = lax.psum_scatter(input_partial, "filt", scatter_dimension=1, tiled=True)
    grad_inputs = grad_rows.astype(jnp.bfloat16)
    depth = planes * count
    grad_two = weight_terms(both[0], out_all, depth, height, columns, factor)
    grad_one = weight_terms(both[1], pre_all, depth, height, columns, factor)
    return (grad_inputs, grad_one, grad_two)


def solution(mesh):
    placed = (
        P("space", None, None, None),
        P("space", None, None, None),
        P(None, None, None, None, "filt"),
        P(None, None, None, None, "filt"),
        P("space", None, None, "filt"),
    )
    return jax.shard_map(
        shards,
        mesh=mesh,
        in_specs=placed,
        out_specs=(
            P("space", "filt", None, None),
            P("space", None, None, None, "filt"),
            P("space", None, None, None, "filt"),
        ),
        check_vma=False,
    )
```

profile of v0, /device:TPU:0, one launch (start us, length us, event | category | flops | bytes accessed | tf_op | source)
XLA Modules:
  0.0 189.9 jit_solution(2208045454308915686)
XLA Ops:
  10.2 7.3 %all-to-all-start = ((bf16[2,8,64,256]{3,2,0,1:T(8,128)(2,1)}), bf16[2,8,64,256]{3,2,0,1:T(8,128)(2,1)}, u32[]{:S(2)}, u32[]{:S(2)}) async-start(bf16[2,8,64,256]{3,2,0,1:T(8,128)(2,1)} %copy.16), calls=%async_computation.1 | async-start | bytes 1048576 | tf_op jit(solution)/shard_map/all_to_all | solution.py:68
  17.6 38.5 %all_gather.6 = bf16[16,4,32,128]{3,2,1,0:T(8,128)(2,1)S(1)} all-gather(bf16[2,4,32,128]{3,2,1,0:T(8,128)(2,1)S(1)} %copy-done.36), channel_id=1, replica_groups=mesh['space'=8,'filt'=4] {'space'}, dimensions={0}, use_global_device_ids=true | all-gather | bytes 589824 | tf_op jit(solution)/shard_map/all_gather | solution.py:63
  57.9 1.1 fusion.162
  59.0 1.1 convolution_add_fusion.51
  60.1 1.1 convolution_add_fusion.50
  61.3 1.1 convolution_add_fusion.49
  67.6 1.0 convolution_add_fusion.26
  69.3 2.2 %pad_slice_fusion.27 = (bf16[16,4,32,128]{3,2,1,0:T(8,128)(2,1)}, bf16[16,4,32,128]{3,2,1,0:T(8,128)(2,1)}, bf16[16,4,32,128]{3,2,1,0:T(8,128)(2,1)}, bf16[16,4,...) fusion(bf16[16,4,32,128]{3,2,1,0:T(8,128)(2,1)S(1)} %all_gather.6), kind=kLoop, calls=%fused_computation.80 | loop fusion | bytes 4194304 | tf_op jit(solution)/shard_map/slice | solution.py:16
  71.5 4.4 %pad_slice_fusion.26 = (bf16[16,4,32,128]{3,2,1,0:T(8,128)(2,1)S(1)}, bf16[16,4,32,128]{3,2,1,0:T(8,128)(2,1)}, bf16[16,4,32,128]{3,2,1,0:T(8,128)(2,1)}, bf16[1...) fusion(bf16[16,4,32,128]{3,2,1,0:T(8,128)(2,1)S(1)} %all_gather.6), kind=kLoop, calls=%fused_computation.79 | loop fusion | bytes 10485760 | tf_op jit(solution)/shard_map/slice | solution.py:16
  75.9 1.2 fusion.218
  77.2 2.0 %fusion.53 = f32[64,27,128]{2,0,1:T(8,128)} fusion(bf16[64,2048]{1,0:T(8,128)(2,1)S(1)} %bitcast.700, bf16[2048,128]{1,0:T(8,128)(2,1)} %bitcast.766), kind=kOutput, calls=%fused_computation.238 | convolution fusion | flops 33562624 | bytes 819200 | tf_op jit(solution)/shard_map/dot_general | solution.py:44
  79.2 1.9 %fusion.51 = f32[64,27,128]{2,0,1:T(8,128)} fusion(f32[64,27,128]{2,0,1:T(8,128)} %fusion.53, bf16[64,2048]{1,0:T(8,128)(2,1)S(1)} %bitcast.701, bf16[2048,128]{1,0:T(8,128)(2,1)} %bitcast.765), kind=kOutput, calls=%fused_computation.235 | convolution fusion | flops 33562624 | bytes 819200 | tf_op jit(solution)/shard_map/dot_general | solution.py:44
  81.1 2.0 %fusion.49 = f32[64,27,128]{2,0,1:T(8,128)} fusion(f32[64,27,128]{2,0,1:T(8,128)} %fusion.51, bf16[64,2048]{1,0:T(8,128)(2,1)S(1)} %bitcast.702, bf16[2048,128]{1,0:T(8,128)(2,1)} %bitcast.764), kind=kOutput, calls=%fused_computation.232 | convolution fusion | flops 33562624 | bytes 819200 | tf_op jit(solution)/shard_map/dot_general | solution.py:44
  104.4 31.5 %all_gather.7 = bf16[16,4,32,128]{3,2,1,0:T(8,128)(2,1)S(1)} all-gather(bf16[2,4,32,128]{3,2,1,0:T(8,128)(2,1)S(1)} %select_convert_fusion), channel_id=1, replica_groups=mesh['space'=8,'filt'=4] {'space'}, dimensions={0}, use_global_device_ids=true | all-gather | bytes 589824 | tf_op jit(solution)/shard_map/all_gather | solution.py:77
  135.8 4.5 %pad_slice_fusion = (bf16[16,4,32,128]{3,2,1,0:T(8,128)(2,1)S(1)}, bf16[16,4,32,128]{3,2,1,0:T(8,128)(2,1)}, bf16[16,4,32,128]{3,2,1,0:T(8,128)(2,1)}, bf16[16,4...) fusion(bf16[16,4,32,128]{3,2,1,0:T(8,128)(2,1)S(1)} %all_gather.7), kind=kLoop, calls=%fused_computation.26 | loop fusion | bytes 10485760 | tf_op jit(solution)/shard_map/slice | solution.py:16
  140.3 2.2 %pad_slice_fusion.1 = (bf16[16,4,32,128]{3,2,1,0:T(8,128)(2,1)}, bf16[16,4,32,128]{3,2,1,0:T(8,128)(2,1)}, bf16[16,4,32,128]{3,2,1,0:T(8,128)(2,1)}, bf16[16,4,3...) fusion(bf16[16,4,32,128]{3,2,1,0:T(8,128)(2,1)S(1)} %all_gather.7), kind=kLoop, calls=%fused_computation.27 | loop fusion | bytes 4194304 | tf_op jit(solution)/shard_map/slice | solution.py:16
  150.4 1.0 convolution_add_fusion
  151.4 17.4 %all-reduce.4 = bf16[2,4,32,512]{3,2,1,0:T(8,128)(2,1)} all-reduce(f32[2,4,32,512]{3,2,1,0:T(8,128)} %bitcast.768), channel_id=3, replica_groups=mesh['space'=8,'filt'=4] {'filt'}, use_global_device_ids=true, to_apply=%region_1.2.clone | all-reduce | flops 131072 | bytes 786432
  168.8 1.4 fusion.107
  170.3 1.3 fusion.105
  171.6 1.3 fusion.103
  172.9 1.3 fusion.101
  174.3 1.3 fusion.99
  180.9 2.1 %dynamic-slice_convert_fusion = bf16[2,1,32,512]{3,2,1,0:T(8,128)(2,1)} fusion(bf16[2,4,32,512]{3,2,1,0:T(8,128)(2,1)} %all-reduce.4, u32[]{:T(128)} %bitcast.231), kind=kLoop, calls=%fused_computation.321 | loop fusion | bytes 131076 | tf_op jit(solution)/shard_map/convert_element_type | solution.py:81
  (188 shorter events, 44.5 us)
Async XLA Ops:
  7.2 10.4 %copy-start.36 = (bf16[2,4,32,128]{3,2,1,0:T(8,128)(2,1)S(1)}, bf16[2,4,32,128]{3,2,1,0:T(8,128)(2,1)}, u32[]{:S(2)}) copy-start(bf16[2,4,32,128]{3,2,1,0:T(8,128)(2,1)} %param.9) | copy-start | bytes 196612
  10.2 65.7 %all-to-all-start = ((bf16[2,8,64,256]{3,2,0,1:T(8,128)(2,1)}), bf16[2,8,64,256]{3,2,0,1:T(8,128)(2,1)}, u32[]{:S(2)}, u32[]{:S(2)}) async-start(bf16[2,8,64,256]{3,2,0,1:T(8,128)(2,1)} %copy.16), calls=%async_computation.1 | async-start | bytes 1048576 | tf_op jit(solution)/shard_map/all_to_all | solution.py:68
  17.5 85.9 %reduce-scatter.5.cloned.1.call-start = ((), (), s32[]{:S(2)}) async-start(), calls=%async_computation.2 | async-start | bytes 655360 | tf_op jit(solution)/shard_map/reduce_scatter | solution.py:71
  75.9 7.2 %copy-start.21 = (bf16[16,4,32,128]{3,2,1,0:T(8,128)(2,1)S(1)}, bf16[16,4,32,128]{3,2,1,0:T(8,128)(2,1)}, u32[]{:S(2)}) copy-start(bf16[16,4,32,128]{3,2,1,0:T(8,128)(2,1)} %get-tuple-element.7) | copy-start | bytes 1572868
  75.9 8.1 %copy-start.20 = (bf16[16,4,32,128]{3,2,1,0:T(8,128)(2,1)S(1)}, bf16[16,4,32,128]{3,2,1,0:T(8,128)(2,1)}, u32[]{:S(2)}) copy-start(bf16[16,4,32,128]{3,2,1,0:T(8,128)(2,1)} %get-tuple-element.8) | copy-start | bytes 1572868
  75.9 8.9 %copy-start.19 = (bf16[16,4,32,128]{3,2,1,0:T(8,128)(2,1)S(1)}, bf16[16,4,32,128]{3,2,1,0:T(8,128)(2,1)}, u32[]{:S(2)}) copy-start(bf16[16,4,32,128]{3,2,1,0:T(8,128)(2,1)} %get-tuple-element.9) | copy-start | bytes 1572868
  75.9 9.7 %copy-start.18 = (bf16[16,4,32,128]{3,2,1,0:T(8,128)(2,1)S(1)}, bf16[16,4,32,128]{3,2,1,0:T(8,128)(2,1)}, u32[]{:S(2)}) copy-start(bf16[16,4,32,128]{3,2,1,0:T(8,128)(2,1)} %get-tuple-element.10) | copy-start | bytes 1572868
  75.9 10.6 %copy-start.17 = (bf16[16,4,32,128]{3,2,1,0:T(8,128)(2,1)S(1)}, bf16[16,4,32,128]{3,2,1,0:T(8,128)(2,1)}, u32[]{:S(2)}) copy-start(bf16[16,4,32,128]{3,2,1,0:T(8,128)(2,1)} %get-tuple-element.11) | copy-start | bytes 1572868
  77.2 10.2 %copy-start.16 = (bf16[16,4,32,128]{3,2,1,0:T(8,128)(2,1)S(1)}, bf16[16,4,32,128]{3,2,1,0:T(8,128)(2,1)}, u32[]{:S(2)}) copy-start(bf16[16,4,32,128]{3,2,1,0:T(8,128)(2,1)} %get-tuple-element.12) | copy-start | bytes 1572868
  77.2 11.0 %copy-start.15 = (bf16[16,4,32,128]{3,2,1,0:T(8,128)(2,1)S(1)}, bf16[16,4,32,128]{3,2,1,0:T(8,128)(2,1)}, u32[]{:S(2)}) copy-start(bf16[16,4,32,128]{3,2,1,0:T(8,128)(2,1)} %get-tuple-element.13) | copy-start | bytes 1572868
  79.2 9.9 %copy-start.14 = (bf16[16,4,32,128]{3,2,1,0:T(8,128)(2,1)S(1)}, bf16[16,4,32,128]{3,2,1,0:T(8,128)(2,1)}, u32[]{:S(2)}) copy-start(bf16[16,4,32,128]{3,2,1,0:T(8,128)(2,1)} %get-tuple-element.14) | copy-start | bytes 1572868
  81.1 8.7 %copy-start.13 = (bf16[16,4,32,128]{3,2,1,0:T(8,128)(2,1)S(1)}, bf16[16,4,32,128]{3,2,1,0:T(8,128)(2,1)}, u32[]{:S(2)}) copy-start(bf16[16,4,32,128]{3,2,1,0:T(8,128)(2,1)} %get-tuple-element.15) | copy-start | bytes 1572868
  83.1 7.6 %copy-start.12 = (bf16[16,4,32,128]{3,2,1,0:T(8,128)(2,1)S(1)}, bf16[16,4,32,128]{3,2,1,0:T(8,128)(2,1)}, u32[]{:S(2)}) copy-start(bf16[16,4,32,128]{3,2,1,0:T(8,128)(2,1)} %get-tuple-element.16) | copy-start | bytes 1572868
  84.8 7.6 %copy-start.11 = (bf16[16,4,32,128]{3,2,1,0:T(8,128)(2,1)S(1)}, bf16[16,4,32,128]{3,2,1,0:T(8,128)(2,1)}, u32[]{:S(2)}) copy-start(bf16[16,4,32,128]{3,2,1,0:T(8,128)(2,1)} %get-tuple-element.17) | copy-start | bytes 1572868
  89.0 7.6 %copy-start.35 = (bf16[16,4,32,128]{3,2,1,0:T(8,128)(2,1)S(1)}, bf16[16,4,32,128]{3,2,1,0:T(8,128)(2,1)}, u32[]{:S(2)}) copy-start(bf16[16,4,32,128]{3,2,1,0:T(8,128)(2,1)} %get-tuple-element.23) | copy-start | bytes 1572868
  89.9 7.6 %copy-start.34 = (bf16[16,4,32,128]{3,2,1,0:T(8,128)(2,1)S(1)}, bf16[16,4,32,128]{3,2,1,0:T(8,128)(2,1)}, u32[]{:S(2)}) copy-start(bf16[16,4,32,128]{3,2,1,0:T(8,128)(2,1)} %get-tuple-element.24) | copy-start | bytes 1572868
  90.7 7.6 %copy-start.33 = (bf16[16,4,32,128]{3,2,1,0:T(8,128)(2,1)S(1)}, bf16[16,4,32,128]{3,2,1,0:T(8,128)(2,1)}, u32[]{:S(2)}) copy-start(bf16[16,4,32,128]{3,2,1,0:T(8,128)(2,1)} %get-tuple-element.25) | copy-start | bytes 1572868
  91.6 7.6 %copy-start.32 = (bf16[16,4,32,128]{3,2,1,0:T(8,128)(2,1)S(1)}, bf16[16,4,32,128]{3,2,1,0:T(8,128)(2,1)}, u32[]{:S(2)}) copy-start(bf16[16,4,32,128]{3,2,1,0:T(8,128)(2,1)} %get-tuple-element.26) | copy-start | bytes 1572868
  93.3 6.8 %copy-start.31 = (bf16[16,4,32,128]{3,2,1,0:T(8,128)(2,1)S(1)}, bf16[16,4,32,128]{3,2,1,0:T(8,128)(2,1)}, u32[]{:S(2)}) copy-start(bf16[16,4,32,128]{3,2,1,0:T(8,128)(2,1)} %get-tuple-element.27) | copy-start | bytes 1572868
  94.1 6.8 %copy-start.30 = (bf16[16,4,32,128]{3,2,1,0:T(8,128)(2,1)S(1)}, bf16[16,4,32,128]{3,2,1,0:T(8,128)(2,1)}, u32[]{:S(2)}) copy-start(bf16[16,4,32,128]{3,2,1,0:T(8,128)(2,1)} %get-tuple-element.28) | copy-start | bytes 1572868
  168.8 6.9 %copy-start.9 = (bf16[16,4,32,128]{3,2,1,0:T(8,128)(2,1)S(1)}, bf16[16,4,32,128]{3,2,1,0:T(8,128)(2,1)}, u32[]{:S(2)}) copy-start(bf16[16,4,32,128]{3,2,1,0:T(8,128)(2,1)} %get-tuple-element.38) | copy-start | bytes 1572868
  168.8 7.2 %copy-start.8 = (bf16[16,4,32,128]{3,2,1,0:T(8,128)(2,1)S(1)}, bf16[16,4,32,128]{3,2,1,0:T(8,128)(2,1)}, u32[]{:S(2)}) copy-start(bf16[16,4,32,128]{3,2,1,0:T(8,128)(2,1)} %get-tuple-element.39) | copy-start | bytes 1572868
  168.8 7.4 %copy-start.7 = (bf16[16,4,32,128]{3,2,1,0:T(8,128)(2,1)S(1)}, bf16[16,4,32,128]{3,2,1,0:T(8,128)(2,1)}, u32[]{:S(2)}) copy-start(bf16[16,4,32,128]{3,2,1,0:T(8,128)(2,1)} %get-tuple-element.40) | copy-start | bytes 1572868
  168.8 7.7 %copy-start.6 = (bf16[16,4,32,128]{3,2,1,0:T(8,128)(2,1)S(1)}, bf16[16,4,32,128]{3,2,1,0:T(8,128)(2,1)}, u32[]{:S(2)}) copy-start(bf16[16,4,32,128]{3,2,1,0:T(8,128)(2,1)} %get-tuple-element.41) | copy-start | bytes 1572868
  (17 other events, 61.6 us)
Sparse Core Ops, SparseCore 0:
  68.8 18.9 reduce-scatter.4
where the time goes:
time: 191 us; the launch traced here: 190 us
  blocking collectives  87.4 us (46%)
  matrix products  55.3 us (29%)
  local copies, waits for them, and re-layouts  21.9 us (11%)
  between operations  15 us (8%)
  starting transfers between devices  7.32 us (4%)
  other arithmetic  2.93 us (2%)
    all_gather x1, blocking collectives, shards(): out_all = pad_all(lax.all_gather(grad_out, 'space', axis=0, tiled=True))  38.5 us
    dot_general x54, matrix products, weight_terms(): lax.dot_general(source, window, (((1,), (0,)), ((), ())), preferred_eleme...  37.7 us
    all_gather x1, blocking collectives, shards(): pre_all = pad_all(lax.all_gather(grad_pre, 'space', axis=0, tiled=True))  31.5 us
    dot_general x54, matrix products, carry_back(): lax.dot_general(window, weight[:, tap[0], tap[1], tap[2], :], (((1,), (1,...  17.5 us
    unnamed x1, blocking collectives  17.4 us
    slice x8, local copies, waits for them, and re-layouts, window_at(): padded[2 - tap[0]:2 - tap[0] + planes, 2 - tap[1]:2 - tap[1] + height, 2...  16.7 us
    all_to_all x1, starting transfers between devices, shards(): both = lax.all_to_all(both, 'space', 1, 1)  7.28 us
  transfers between devices with their start and end apart: 2, of which 0 were waited for; matrix products, arithmetic and copies ran while one was open for 25% of the time, Pallas kernels for 0%

commit v1 on v0

--- a/solution.py
+++ b/solution.py
@@ -10,6 +10,18 @@
     for tap_row in range(3)
     for tap_col in range(3)
 ]
+
+
+def collect(value, axis, dim):
+    ways, here, hop = (lax.axis_size(axis), lax.axis_index(axis), value.shape[dim])
+    line, have = (value, 1)
+    while have < ways:
+        line = jnp.concatenate(
+            [line, lax.ppermute(line, axis, [(d, (d - have) % ways) for d in range(ways)])],
+            axis=dim,
+        )
+        have = 2 * have
+    return jnp.roll(line, here * hop, axis=dim)
 
 
 def window_at(padded, tap, planes, height, columns):
@@ -74,7 +86,7 @@
         pre_hidden, lax.axis_index("filt") * group_width, group_width, 3
     )
     grad_pre = jnp.where(own_pre > 0, grad_hidden, jnp.zeros_like(grad_hidden)).astype(jnp.bfloat16)
-    pre_all = pad_all(lax.all_gather(grad_pre, "space", axis=0, tiled=True))
+    pre_all = pad_all(collect(grad_pre, "space", 0))
     pre_pad = lax.dynamic_slice_in_dim(pre_all, start, planes + 2, 0)
     input_partial = carry_back(pre_pad, weight_one, planes, height, columns)
     grad_rows = lax.psum_scatter(input_partial, "filt", scatter_dimension=1, tiled=True)

time: 191 us -> 178 us (0.932)
  blocking collectives: 87.4 us -> 56.2 us
  waiting for transfers between devices: 0.02 us -> 17.4 us
    all_gather x1 -> x0, blocking collectives: 31.5 us -> none  [shards(): pre_all = pad_all(lax.all_gather(grad_pre, 'space', axis=0, tiled=True))]
    ppermute x0 -> x3, waiting for transfers between devices: none -> 17.3 us  [collect(): lax.ppermute(line, axis, [(d, (d - have) % ways) for d in range(ways)])]
  transfers between devices with their start and end apart: 2 -> 5, of which waited for: 0 -> 3; matrix products, arithmetic and copies ran while one was open for 25% -> 27% of each run, Pallas kernels for 0% -> 0%
where the time goes in v1:
time: 178 us
  blocking collectives  56.2 us (32%)
  matrix products  55.3 us (31%)
  local copies, waits for them, and re-layouts  22.4 us (13%)
  waiting for transfers between devices  17.4 us (10%)
  between operations  15.1 us (8%)
  starting transfers between devices  8.28 us (5%)
  other arithmetic  2.98 us (2%)
    all_gather x1, blocking collectives, shards(): out_all = pad_all(lax.all_gather(grad_out, 'space', axis=0, tiled=True))  38.5 us
    dot_general x54, matrix products, weight_terms(): lax.dot_general(source, window, (((1,), (0,)), ((), ())), preferred_eleme...  37.7 us
    unnamed x1, blocking collectives  17.6 us
    dot_general x54, matrix products, carry_back(): lax.dot_general(window, weight[:, tap[0], tap[1], tap[2], :], (((1,), (1,...  17.5 us
    ppermute x3, waiting for transfers between devices, collect(): lax.ppermute(line, axis, [(d, (d - have) % ways) for d in range(ways)])  17.3 us
    slice x8, local copies, waits for them, and re-layouts, window_at(): padded[2 - tap[0]:2 - tap[0] + planes, 2 - tap[1]:2 - tap[1] + height, 2...  16.3 us
    all_to_all x1, starting transfers between devices, shards(): both = lax.all_to_all(both, 'space', 1, 1)  7.28 us
  transfers between devices with their start and end apart: 5, of which 3 were waited for; matrix products, arithmetic and copies ran while one was open for 27% of the time, Pallas kernels for 0%

profile of v1, /device:TPU:0, one launch (start us, length us, event | category | flops | bytes accessed | tf_op | source)
XLA Modules:
  0.0 177.6 jit_solution(17445497335372553836)
XLA Ops:
  10.2 7.3 %all-to-all-start = ((bf16[2,8,64,256]{3,2,0,1:T(8,128)(2,1)}), bf16[2,8,64,256]{3,2,0,1:T(8,128)(2,1)}, u32[]{:S(2)}, u32[]{:S(2)}) async-start(bf16[2,8,64,256]{3,2,0,1:T(8,128)(2,1)} %copy.16), calls=%async_computation.1 | async-start | bytes 1048576 | tf_op jit(solution)/shard_map/all_to_all | solution.py:80
  17.6 38.5 %all_gather.3 = bf16[16,4,32,128]{3,2,1,0:T(8,128)(2,1)S(1)} all-gather(bf16[2,4,32,128]{3,2,1,0:T(8,128)(2,1)S(1)} %copy-done.37), channel_id=1, replica_groups=mesh['space'=8,'filt'=4] {'space'}, dimensions={0}, use_global_device_ids=true | all-gather | bytes 589824 | tf_op jit(solution)/shard_map/all_gather | solution.py:75
  57.9 1.1 fusion.162
  59.0 1.1 convolution_add_fusion.51
  60.1 1.1 convolution_add_fusion.50
  61.3 1.1 convolution_add_fusion.49
  69.3 2.2 %pad_slice_fusion.27 = (bf16[16,4,32,128]{3,2,1,0:T(8,128)(2,1)}, bf16[16,4,32,128]{3,2,1,0:T(8,128)(2,1)}, bf16[16,4,32,128]{3,2,1,0:T(8,128)(2,1)}, bf16[16,4,...) fusion(bf16[16,4,32,128]{3,2,1,0:T(8,128)(2,1)S(1)} %all_gather.3), kind=kLoop, calls=%fused_computation.80 | loop fusion | bytes 4194304 | tf_op jit(solution)/shard_map/slice | solution.py:28
  71.5 4.2 %pad_slice_fusion.26 = (bf16[16,4,32,128]{3,2,1,0:T(8,128)(2,1)S(1)}, bf16[16,4,32,128]{3,2,1,0:T(8,128)(2,1)}, bf16[16,4,32,128]{3,2,1,0:T(8,128)(2,1)}, bf16[1...) fusion(bf16[16,4,32,128]{3,2,1,0:T(8,128)(2,1)S(1)} %all_gather.3), kind=kLoop, calls=%fused_computation.79 | loop fusion | bytes 10485760 | tf_op jit(solution)/shard_map/slice | solution.py:28
  75.8 1.9 %fusion.218 = (bf16[1,64,8,256]{3,1,0,2:T(8,128)(2,1)S(1)}, bf16[1,64,8,256]{3,1,0,2:T(8,128)(2,1)}) fusion(bf16[2,64,8,256]{3,1,0,2:T(8,128)(2,1)} %bitcast.114), kind=kLoop, calls=%fused_computation.445 | loop fusion | bytes 1048576 | tf_op jit(solution)/shard_map/slice | solution.py:95
  77.8 2.0 %fusion.53 = f32[64,27,128]{2,0,1:T(8,128)} fusion(bf16[64,2048]{1,0:T(8,128)(2,1)S(1)} %bitcast.700, bf16[2048,128]{1,0:T(8,128)(2,1)} %bitcast.766), kind=kOutput, calls=%fused_computation.238 | convolution fusion | flops 33562624 | bytes 819200 | tf_op jit(solution)/shard_map/dot_general | solution.py:56
  79.7 1.9 %fusion.51 = f32[64,27,128]{2,0,1:T(8,128)} fusion(f32[64,27,128]{2,0,1:T(8,128)} %fusion.53, bf16[64,2048]{1,0:T(8,128)(2,1)S(1)} %bitcast.701, bf16[2048,128]{1,0:T(8,128)(2,1)} %bitcast.765), kind=kOutput, calls=%fused_computation.235 | convolution fusion | flops 33562624 | bytes 819200 | tf_op jit(solution)/shard_map/dot_general | solution.py:56
  81.7 1.9 %fusion.49 = f32[64,27,128]{2,0,1:T(8,128)} fusion(f32[64,27,128]{2,0,1:T(8,128)} %fusion.51, bf16[64,2048]{1,0:T(8,128)(2,1)S(1)} %bitcast.702, bf16[2048,128]{1,0:T(8,128)(2,1)} %bitcast.764), kind=kOutput, calls=%fused_computation.232 | convolution fusion | flops 33562624 | bytes 819200 | tf_op jit(solution)/shard_map/dot_general | solution.py:56
  103.3 3.4 %collective-permute-done = bf16[2,4,32,128]{3,2,1,0:T(8,128)(2,1)S(1)} collective-permute-done((bf16[2,4,32,128]{3,2,1,0:T(8,128)(2,1)S(1)}, bf16[2,4,32,128]{3,2,1,0:T(8,128)(2,1)S(1)}, u32[]{:S(2)}, u32[]{:S(2)}) %collective-permute-start) | collective-permute-done | bytes 65568 | tf_op jit(solution)/shard_map/ppermute | solution.py:20
  108.4 5.8 %collective-permute-done.1 = bf16[4,4,32,128]{3,2,1,0:T(8,128)(2,1)S(1)} collective-permute-done((bf16[4,4,32,128]{3,2,1,0:T(8,128)(2,1)S(1)}, bf16[4,4,32,128]{3,2,1,0:T(8,128)(2,1)S(1)}, u32[]{:S(2)}, u32[]{:S(2)}) %collective-permute-start.1) | collective-permute-done | bytes 131104 | tf_op jit(solution)/shard_map/ppermute | solution.py:20
  115.2 8.2 %collective-permute-done.2 = bf16[8,4,32,128]{3,2,1,0:T(8,128)(2,1)S(1)} collective-permute-done((bf16[8,4,32,128]{3,2,1,0:T(8,128)(2,1)S(1)}, bf16[8,4,32,128]{3,2,1,0:T(8,128)(2,1)S(1)}, u32[]{:S(2)}, u32[]{:S(2)}) %collective-permute-start.2) | collective-permute-done | bytes 262176 | tf_op jit(solution)/shard_map/ppermute | solution.py:20
  123.5 4.3 %pad_slice_fusion = (bf16[16,4,32,128]{3,2,1,0:T(8,128)(2,1)S(1)}, bf16[16,4,32,128]{3,2,1,0:T(8,128)(2,1)}, bf16[16,4,32,128]{3,2,1,0:T(8,128)(2,1)}, bf16[16,4...) fusion(bf16[16,4,32,128]{3,2,1,0:T(8,128)(2,1)S(1)} %constant_d, ...), kind=kLoop, calls=%fused_computation.26 | loop fusion | bytes 10485760 | tf_op jit(solution)/shard_map/slice | solution.py:28
  127.8 2.2 %pad_slice_fusion.1 = (bf16[16,4,32,128]{3,2,1,0:T(8,128)(2,1)}, bf16[16,4,32,128]{3,2,1,0:T(8,128)(2,1)}, bf16[16,4,32,128]{3,2,1,0:T(8,128)(2,1)}, bf16[16,4,3...) fusion(bf16[16,4,32,128]{3,2,1,0:T(8,128)(2,1)S(1)} %constant_d, ...), kind=kLoop, calls=%fused_computation.27 | loop fusion | bytes 4194304 | tf_op jit(solution)/shard_map/slice | solution.py:28
  138.9 17.6 %all-reduce.4 = bf16[2,4,32,512]{3,2,1,0:T(8,128)(2,1)} all-reduce(f32[2,4,32,512]{3,2,1,0:T(8,128)} %bitcast.768), channel_id=3, replica_groups=mesh['space'=8,'filt'=4] {'filt'}, use_global_device_ids=true, to_apply=%region_1.2.clone | all-reduce | flops 131072 | bytes 786432
  156.6 1.4 fusion.107
  158.0 1.3 fusion.105
  159.3 1.3 fusion.103
  160.7 1.3 fusion.101
  162.0 1.3 fusion.99
  168.6 2.1 %dynamic-slice_convert_fusion = bf16[2,1,32,512]{3,2,1,0:T(8,128)(2,1)} fusion(bf16[2,4,32,512]{3,2,1,0:T(8,128)(2,1)} %all-reduce.4, u32[]{:T(128)} %bitcast.231), kind=kLoop, calls=%fused_computation.323 | loop fusion | bytes 131076 | tf_op jit(solution)/shard_map/convert_element_type | solution.py:93
  (205 shorter events, 47.8 us)
Async XLA Ops:
  7.2 10.4 %copy-start.37 = (bf16[2,4,32,128]{3,2,1,0:T(8,128)(2,1)S(1)}, bf16[2,4,32,128]{3,2,1,0:T(8,128)(2,1)}, u32[]{:S(2)}) copy-start(bf16[2,4,32,128]{3,2,1,0:T(8,128)(2,1)} %param.9) | copy-start | bytes 196612
  10.2 65.5 %all-to-all-start = ((bf16[2,8,64,256]{3,2,0,1:T(8,128)(2,1)}), bf16[2,8,64,256]{3,2,0,1:T(8,128)(2,1)}, u32[]{:S(2)}, u32[]{:S(2)}) async-start(bf16[2,8,64,256]{3,2,0,1:T(8,128)(2,1)} %copy.16), calls=%async_computation.1 | async-start | bytes 1048576 | tf_op jit(solution)/shard_map/all_to_all | solution.py:80
  17.5 83.9 %reduce-scatter.5.cloned.1.call-start = ((), (), s32[]{:S(2)}) async-start(), calls=%async_computation.2 | async-start | bytes 655360 | tf_op jit(solution)/shard_map/reduce_scatter | solution.py:83
  75.8 7.9 %copy-start.21 = (bf16[16,4,32,128]{3,2,1,0:T(8,128)(2,1)S(1)}, bf16[16,4,32,128]{3,2,1,0:T(8,128)(2,1)}, u32[]{:S(2)}) copy-start(bf16[16,4,32,128]{3,2,1,0:T(8,128)(2,1)} %get-tuple-element.9) | copy-start | bytes 1572868
  75.8 8.7 %copy-start.20 = (bf16[16,4,32,128]{3,2,1,0:T(8,128)(2,1)S(1)}, bf16[16,4,32,128]{3,2,1,0:T(8,128)(2,1)}, u32[]{:S(2)}) copy-start(bf16[16,4,32,128]{3,2,1,0:T(8,128)(2,1)} %get-tuple-element.10) | copy-start | bytes 1572868
  75.8 9.5 %copy-start.19 = (bf16[16,4,32,128]{3,2,1,0:T(8,128)(2,1)S(1)}, bf16[16,4,32,128]{3,2,1,0:T(8,128)(2,1)}, u32[]{:S(2)}) copy-start(bf16[16,4,32,128]{3,2,1,0:T(8,128)(2,1)} %get-tuple-element.11) | copy-start | bytes 1572868
  75.8 10.4 %copy-start.18 = (bf16[16,4,32,128]{3,2,1,0:T(8,128)(2,1)S(1)}, bf16[16,4,32,128]{3,2,1,0:T(8,128)(2,1)}, u32[]{:S(2)}) copy-start(bf16[16,4,32,128]{3,2,1,0:T(8,128)(2,1)} %get-tuple-element.12) | copy-start | bytes 1572868
  75.8 11.2 %copy-start.17 = (bf16[16,4,32,128]{3,2,1,0:T(8,128)(2,1)S(1)}, bf16[16,4,32,128]{3,2,1,0:T(8,128)(2,1)}, u32[]{:S(2)}) copy-start(bf16[16,4,32,128]{3,2,1,0:T(8,128)(2,1)} %get-tuple-element.13) | copy-start | bytes 1572868
  77.7 10.1 %copy-start.16 = (bf16[16,4,32,128]{3,2,1,0:T(8,128)(2,1)S(1)}, bf16[16,4,32,128]{3,2,1,0:T(8,128)(2,1)}, u32[]{:S(2)}) copy-start(bf16[16,4,32,128]{3,2,1,0:T(8,128)(2,1)} %get-tuple-element.14) | copy-start | bytes 1572868
  77.8 11.0 %copy-start.15 = (bf16[16,4,32,128]{3,2,1,0:T(8,128)(2,1)S(1)}, bf16[16,4,32,128]{3,2,1,0:T(8,128)(2,1)}, u32[]{:S(2)}) copy-start(bf16[16,4,32,128]{3,2,1,0:T(8,128)(2,1)} %get-tuple-element.15) | copy-start | bytes 1572868
  79.7 9.8 %copy-start.14 = (bf16[16,4,32,128]{3,2,1,0:T(8,128)(2,1)S(1)}, bf16[16,4,32,128]{3,2,1,0:T(8,128)(2,1)}, u32[]{:S(2)}) copy-start(bf16[16,4,32,128]{3,2,1,0:T(8,128)(2,1)} %get-tuple-element.16) | copy-start | bytes 1572868
  81.7 8.7 %copy-start.13 = (bf16[16,4,32,128]{3,2,1,0:T(8,128)(2,1)S(1)}, bf16[16,4,32,128]{3,2,1,0:T(8,128)(2,1)}, u32[]{:S(2)}) copy-start(bf16[16,4,32,128]{3,2,1,0:T(8,128)(2,1)} %get-tuple-element.17) | copy-start | bytes 1572868
  83.6 7.6 %copy-start.12 = (bf16[16,4,32,128]{3,2,1,0:T(8,128)(2,1)S(1)}, bf16[16,4,32,128]{3,2,1,0:T(8,128)(2,1)}, u32[]{:S(2)}) copy-start(bf16[16,4,32,128]{3,2,1,0:T(8,128)(2,1)} %get-tuple-element.18) | copy-start | bytes 1572868
  85.3 7.6 %copy-start.11 = (bf16[16,4,32,128]{3,2,1,0:T(8,128)(2,1)S(1)}, bf16[16,4,32,128]{3,2,1,0:T(8,128)(2,1)}, u32[]{:S(2)}) copy-start(bf16[16,4,32,128]{3,2,1,0:T(8,128)(2,1)} %get-tuple-element.19) | copy-start | bytes 1572868
  89.6 7.6 %copy-start.35 = (bf16[16,4,32,128]{3,2,1,0:T(8,128)(2,1)S(1)}, bf16[16,4,32,128]{3,2,1,0:T(8,128)(2,1)}, u32[]{:S(2)}) copy-start(bf16[16,4,32,128]{3,2,1,0:T(8,128)(2,1)} %get-tuple-element.25) | copy-start | bytes 1572868
  92.1 7.6 %copy-start.32 = (bf16[16,4,32,128]{3,2,1,0:T(8,128)(2,1)S(1)}, bf16[16,4,32,128]{3,2,1,0:T(8,128)(2,1)}, u32[]{:S(2)}) copy-start(bf16[16,4,32,128]{3,2,1,0:T(8,128)(2,1)} %get-tuple-element.28) | copy-start | bytes 1572868
  93.0 7.6 %copy-start.31 = (bf16[16,4,32,128]{3,2,1,0:T(8,128)(2,1)S(1)}, bf16[16,4,32,128]{3,2,1,0:T(8,128)(2,1)}, u32[]{:S(2)}) copy-start(bf16[16,4,32,128]{3,2,1,0:T(8,128)(2,1)} %get-tuple-element.29) | copy-start | bytes 1572868
  94.6 7.8 %copy-start.30 = (bf16[16,4,32,128]{3,2,1,0:T(8,128)(2,1)S(1)}, bf16[16,4,32,128]{3,2,1,0:T(8,128)(2,1)}, u32[]{:S(2)}) copy-start(bf16[16,4,32,128]{3,2,1,0:T(8,128)(2,1)} %get-tuple-element.30) | copy-start | bytes 1572868
  95.5 12.0 %copy-start.29 = (bf16[16,4,32,128]{3,2,1,0:T(8,128)(2,1)S(1)}, bf16[16,4,32,128]{3,2,1,0:T(8,128)(2,1)}, u32[]{:S(2)}) copy-start(bf16[16,4,32,128]{3,2,1,0:T(8,128)(2,1)} %get-tuple-element.24) | copy-start | bytes 1572868
  98.0 17.1 %copy-start.36 = (bf16[1,64,8,256]{3,1,0,2:T(8,128)(2,1)S(1)}, bf16[1,64,8,256]{3,1,0,2:T(8,128)(2,1)}, u32[]{:S(2)}) copy-start(bf16[1,64,8,256]{3,1,0,2:T(8,128)(2,1)} %get-tuple-element.32) | copy-start | bytes 786436
  102.4 4.3 %collective-permute-start = (bf16[2,4,32,128]{3,2,1,0:T(8,128)(2,1)S(1)}, bf16[2,4,32,128]{3,2,1,0:T(8,128)(2,1)S(1)}, u32[]{:S(2)}, u32[]{:S(2)}) collective-permute-start(bf16[2,4,32,128]{3,2,1,0:T(8,128)(2,1)S(1)} %get-tuple-element.4), channel_id=1, source_target_pairs={{0,28},{4,0},{8,4},{12,8},{16,12},{20,16},{24,20},{28,24},{1,29},{... | collective-permute-start | bytes 196616 | tf_op jit(solution)/shard_map/ppermute | solution.py:20
  106.7 7.4 %collective-permute-start.1 = (bf16[4,4,32,128]{3,2,1,0:T(8,128)(2,1)S(1)}, bf16[4,4,32,128]{3,2,1,0:T(8,128)(2,1)S(1)}, u32[]{:S(2)}, u32[]{:S(2)}) collective-permute-start(bf16[4,4,32,128]{3,2,1,0:T(8,128)(2,1)S(1)} %pad_maximum_fusion.1), channel_id=1, source_target_pairs={{0,24},{4,28},{8,0},{12,4},{16,8},{20,12},{24,16},{28,20},{1,25},{... | collective-permute-start | bytes 393224 | tf_op jit(solution)/shard_map/ppermute | solution.py:20
  114.2 9.2 %collective-permute-start.2 = (bf16[8,4,32,128]{3,2,1,0:T(8,128)(2,1)S(1)}, bf16[8,4,32,128]{3,2,1,0:T(8,128)(2,1)S(1)}, u32[]{:S(2)}, u32[]{:S(2)}) collective-permute-start(bf16[8,4,32,128]{3,2,1,0:T(8,128)(2,1)S(1)} %pad_maximum_fusion), channel_id=1, source_target_pairs={{0,16},{4,20},{8,24},{12,28},{16,0},{20,4},{24,8},{28,12},{1,17},{... | collective-permute-start | bytes 786440 | tf_op jit(solution)/shard_map/ppermute | solution.py:20
  156.6 7.7 %copy-start.6 = (bf16[16,4,32,128]{3,2,1,0:T(8,128)(2,1)S(1)}, bf16[16,4,32,128]{3,2,1,0:T(8,128)(2,1)}, u32[]{:S(2)}) copy-start(bf16[16,4,32,128]{3,2,1,0:T(8,128)(2,1)} %get-tuple-element.43) | copy-start | bytes 1572868
  (21 other events, 91.7 us)
Sparse Core Ops, SparseCore 0:
  68.8 18.9 reduce-scatter.4
